TPU v7x, 256 devices: a whole 4x4x8 slice. The times are simulated.
256 devices in a mesh: row: 8 (over z), col: 32 (over y, x, core).
Axes of the slice: x: 4, y: 4, z: 8, core: 2. Of those that a mesh axis runs over, the one named last changes fastest.
Arguments:
- amps: bfloat16 [384, 131072], P('row', 'col'), may hold values from -6 to 6
- integrals: bfloat16 [131072, 8192], P('col', 'row'), may hold values from -0.046875 to 0.046875
- cd_first: int32 [131072], P('col'), may hold values from 0 to 2399
- cd_second: int32 [131072], P('col'), may hold values from 0 to 2399
- ab_first: int32 [8192], P('row'), may hold values from 0 to 2399
- ab_second: int32 [8192], P('row'), may hold values from 0 to 2399
- occ_first: int32 [384], P('col'), may hold values from 0 to 199
- occ_second: int32 [384], P('col'), may hold values from 0 to 199
- virt_irrep: int32 [2400], replicated, may hold values from 0 to 7
- occ_energy: float32 [200], replicated, may hold values from -2 to -0.5
- virt_energy: float32 [2400], replicated, may hold values from 0.2 to 3
Outputs:
- update: float32 [384, 8192], P('col', 'row')
All inputs are finite; a program needn't handle non-finite values.
Results may differ from a plain program's by a relative error of at most 0.0003.
Values may be sent and summed in bfloat16 or wider, within the bound.
No kernel may reach another device: no remote copies, remote signals or barrier semaphores. Data moves between devices by JAX's collectives and lax.ppermute only.
A program may use at most 64 MiB of HBM per device.

v0:
```python
import jax
import jax.numpy as jnp
from jax import lax
from jax.sharding import PartitionSpec as P


def table_lookup(values_table, positions):
    row_width = 64
    row_count = -(-values_table.shape[0] // row_width)
    padded_table = jnp.pad(
        values_table, (0, row_count * row_width - values_table.shape[0])
    ).reshape(row_count, row_width)
    high_hot = (
        (positions // row_width)[:, None] == jnp.arange(row_count, dtype=jnp.int32)[None, :]
    ).astype(jnp.float32)
    low_hot = (
        (positions % row_width)[:, None] == jnp.arange(row_width, dtype=jnp.int32)[None, :]
    ).astype(jnp.float32)
    picked = jnp.dot(
        high_hot, padded_table, precision=lax.Precision.HIGHEST, preferred_element_type=jnp.float32
    )
    return jnp.sum(picked * low_hot, axis=1)


def irrep_of(labels_float, first_orb, second_orb):
    first_label = table_lookup(labels_float, first_orb).astype(jnp.int32)
    second_label = table_lookup(labels_float, second_orb).astype(jnp.int32)
    return jnp.bitwise_xor(first_label, second_label)


def on_device(
    amps,
    integrals,
    cd_first,
    cd_second,
    ab_first,
    ab_second,
    occ_first,
    occ_second,
    virt_irrep,
    occ_energy,
    virt_energy,
):
    labels_float = virt_irrep.astype(jnp.float32)
    irrep_cd = irrep_of(labels_float, cd_first, cd_second)
    irrep_ab = irrep_of(labels_float, ab_first, ab_second)
    masked = jnp.where(irrep_cd[:, None] == irrep_ab[None, :], integrals, jnp.zeros_like(integrals))
    partial_sums = jnp.dot(
        lax.all_gather(amps, "row", axis=0, tiled=True), masked, preferred_element_type=jnp.float32
    )
    own_rows = occ_first.shape[0]
    summed = lax.psum(partial_sums, "col")
    ladder = lax.dynamic_slice_in_dim(summed, lax.axis_index("col") * own_rows, own_rows, 0)
    virt_part = table_lookup(virt_energy, ab_first) + table_lookup(virt_energy, ab_second)
    occ_part = table_lookup(occ_energy, occ_first) + table_lookup(occ_energy, occ_second)
    denom = virt_part[None, :] - occ_part[:, None]
    return ladder / denom


def solution(mesh):
    in_specs = (
        P("row", "col"),
        P("col", "row"),
        P("col"),
        P("col"),
        P("row"),
        P("row"),
        P("col"),
        P("col"),
        P(),
        P(),
        P(),
    )
    out_specs = P("col", "row")
    return jax.shard_map(
        on_device, mesh=mesh, in_specs=in_specs, out_specs=out_specs, check_vma=False
    )
```

profile of v0, /device:TPU:6, one launch (start us, length us, event | category | flops | bytes accessed | tf_op | source)
XLA Modules:
  0.0 190.4 jit_solution(7204045527473177920)
XLA Ops:
  6.5 0.0 all-gather.2.cloned.1.call-start
  6.5 0.7 all-gather.2.cloned.1.call-update
  7.3 0.0 all-reduce.5.cloned.1.call-start
  7.3 0.7 convert_element_type.57
  8.0 0.1 reshape.50
  8.1 0.7 add_select_fusion.5
  8.8 0.6 fusion.8
  9.4 0.7 add_select_fusion.7
  10.1 0.6 fusion.7
  10.7 0.7 add_select_fusion.2
  11.4 0.7 fusion.5
  12.1 0.7 add_select_fusion
  12.8 0.7 fusion.6
  13.5 0.0 copy-start.2
  13.6 0.0 copy-start.1
  13.6 0.0 copy-start
  13.6 0.0 copy-start.3
  13.6 43.5 %all-gather.2.cloned.1.call-done = bf16[384,4096]{1,0:T(8,128)(2,1)} async-done(((bf16[48,4096]{1,0:T(8,128)(2,1)}), bf16[384,4096]{1,0:T(8,128)(2,1)}) %all-gather.2.cloned.1.call-update) | async-done | bytes 3145744 | tf_op jit(solution)/shard_map/all_gather | solution.py:49
  57.1 9.0 %fusion.4 = f32[384,1024]{1,0:T(8,128)} fusion(bf16[384,4096]{1,0:T(8,128)(2,1)} %all-gather.2.cloned.1.call-done, bf16[4096,1024]{1,0:T(8,128)(2,1)} %param.12, s32[1024]{0:T(1024)S(1)} %convert_xor_fusion.1, s32[4096]{0:T(1024)S(1)} %convert_xor_fusion), kind=kOutput, calls=%fused_computation.7 | convolution fusion | flops 3229614080 | bytes 13127680 | tf_op jit(solution)/shard_map/dot_general | solution.py:48
  66.1 0.0 all-reduce.5.cloned.1.call-update
  66.1 0.0 copy-done.2
  66.1 0.0 copy-done.1
  66.2 0.1 reshape.52
  66.2 0.0 copy-done
  66.2 0.1 reshape.51
  66.3 0.3 fusion.11
  66.6 0.0 copy-done.3
  66.6 0.3 fusion.12
  67.0 0.6 fusion.10
  67.5 0.6 fusion.9
  68.1 113.8 %all-reduce.5.cloned.1.call-done = f32[384,1024]{1,0:T(8,128)} async-done(((f32[384,1024]{1,0:T(8,128)}), f32[384,1024]{1,0:T(8,128)}) %all-reduce.5.cloned.1.call-update) | async-done | bytes 1572880 | tf_op jit(solution)/shard_map/psum | solution.py:52
  181.9 1.6 subtract_divide_fusion
  (9 shorter events, 0.1 us)
Async XLA Ops:
  6.5 50.5 %all-gather.2.cloned.1.call-start = ((), (), s32[]{:S(2)}) async-start(), calls=%async_computation | async-start | bytes 3538944 | tf_op jit(solution)/shard_map/all_gather | solution.py:49
  7.3 174.7 %all-reduce.5.cloned.1.call-start = ((), (), s32[]{:S(2)}) async-start(), calls=%async_computation.1 | async-start | bytes 3145728 | tf_op jit(solution)/shard_map/psum | solution.py:52
  13.5 52.5 %copy-start.2 = (s32[12]{0:T(128)S(1)}, s32[12]{0:T(128)}, u32[]{:S(2)}) copy-start(s32[12]{0:T(128)} %param.17) | copy-start | bytes 148
  13.6 52.6 %copy-start.1 = (f32[200]{0:T(256)S(1)}, f32[200]{0:T(256)}, u32[]{:S(2)}) copy-start(f32[200]{0:T(256)} %param.20) | copy-start | bytes 2404
  13.6 52.7 %copy-start = (f32[2400]{0:T(1024)S(1)}, f32[2400]{0:T(1024)}, u32[]{:S(2)}) copy-start(f32[2400]{0:T(1024)} %param.21) | copy-start | bytes 28804
  13.6 53.0 %copy-start.3 = (s32[12]{0:T(128)S(1)}, s32[12]{0:T(128)}, u32[]{:S(2)}) copy-start(s32[12]{0:T(128)} %param.18) | copy-start | bytes 148
Sparse Core Ops, SparseCore 0:
  9.1 47.8 all-gather.1
  66.2 115.6 all-reduce.4
where the time goes:
time: 191 us; the launch traced here: 190 us
  waiting for transfers between devices  158 us (83%)
  between operations  13.5 us (7%)
  matrix products  13.3 us (7%)
  other arithmetic  5.24 us (3%)
    psum x1, waiting for transfers between devices, on_device(): summed = lax.psum(partial_sums, 'col')  114 us
    all_gather x1, waiting for transfers between devices, on_device(): lax.all_gather(amps, 'row', axis=0, tiled=True)  43.5 us
    dot_general x1, matrix products, on_device(): jnp.dot(lax.all_gather(amps, 'row', axis=0, tiled=True), masked, preferre...  9 us
    dot_general x8, matrix products, table_lookup(): jnp.dot(high_hot, padded_table, precision=lax.Precision.HIGHEST, preferre...  4.28 us
  transfers between devices with their start and end apart: 2, of which 2 were waited for; matrix products, arithmetic and copies ran while one was open for 4% of the time, Pallas kernels for 0%

commit v1 on v0

--- a/solution.py
+++ b/solution.py
@@ -49,7 +49,9 @@
         lax.all_gather(amps, "row", axis=0, tiled=True), masked, preferred_element_type=jnp.float32
     )
     own_rows = occ_first.shape[0]
-    summed = lax.psum(partial_sums, "col")
+    summed = partial_sums
+    for hop in (1, 2, 4, 8, 16):
+        summed = summed + lax.ppermute(summed, "col", [(dev, dev ^ hop) for dev in range(32)])
     ladder = lax.dynamic_slice_in_dim(summed, lax.axis_index("col") * own_rows, own_rows, 0)
     virt_part = table_lookup(virt_energy, ab_first) + table_lookup(virt_energy, ab_second)
     occ_part = table_lookup(occ_energy, occ_first) + table_lookup(occ_energy, occ_second)

time: 191 us -> 222 us (1.16)
  waiting for transfers between devices: 158 us -> 183 us
  starting transfers between devices: 0.04 us -> 7.27 us
    ppermute x0 -> x5, waiting for transfers between devices: none -> 138 us  [on_device(): lax.ppermute(summed, 'col', [(dev, dev ^ hop) for dev in range(32)])]
    psum x1 -> x0, waiting for transfers between devices: 114 us -> none  [on_device(): summed = lax.psum(partial_sums, 'col')]
    ppermute x0 -> x5, starting transfers between devices: none -> 7.27 us  [on_device(): lax.ppermute(summed, 'col', [(dev, dev ^ hop) for dev in range(32)])]
  transfers between devices with their start and end apart: 2 -> 6, of which waited for: 2 -> 6; matrix products, arithmetic and copies ran while one was open for 4% -> 4% of each run, Pallas kernels for 0% -> 0%
where the time goes in v1:
time: 222 us; the launch traced here: 221 us
  waiting for transfers between devices  183 us (82%)
  between operations  13.5 us (6%)
  matrix products  12.1 us (5%)
  starting transfers between devices  7.27 us (3%)
  other arithmetic  5.55 us (2%)
    ppermute x5, waiting for transfers between devices, on_device(): lax.ppermute(summed, 'col', [(dev, dev ^ hop) for dev in range(32)])  138 us
    all_gather x1, waiting for transfers between devices, on_device(): lax.all_gather(amps, 'row', axis=0, tiled=True)  43.6 us
    dot_general x1, matrix products, on_device(): jnp.dot(lax.all_gather(amps, 'row', axis=0, tiled=True), masked, preferre...  7.85 us
    ppermute x5, starting transfers between devices, on_device(): lax.ppermute(summed, 'col', [(dev, dev ^ hop) for dev in range(32)])  7.27 us
  transfers between devices with their start and end apart: 6, of which 6 were waited for; matrix products, arithmetic and copies ran while one was open for 4% of the time, Pallas kernels for 0%

profile of v1, /device:TPU:6, one launch (start us, length us, event | category | flops | bytes accessed | tf_op | source)
XLA Modules:
  0.0 221.4 jit_solution(10766949934199210422)
XLA Ops:
  6.5 0.7 all-gather.2.cloned.1.call-update
  7.3 0.7 convert_element_type.57
  8.0 0.7 add_select_fusion.5
  8.7 0.6 fusion.8
  9.3 0.7 add_select_fusion.7
  10.0 0.6 fusion.7
  10.6 0.7 add_select_fusion.2
  11.3 0.7 fusion.5
  12.0 0.7 add_select_fusion
  12.8 0.7 fusion.6
  13.5 43.6 %all-gather.2.cloned.1.call-done = bf16[384,4096]{1,0:T(8,128)(2,1)} async-done(((bf16[48,4096]{1,0:T(8,128)(2,1)}), bf16[384,4096]{1,0:T(8,128)(2,1)}) %all-gather.2.cloned.1.call-update) | async-done | bytes 3145744 | tf_op jit(solution)/shard_map/all_gather | solution.py:49
  57.1 7.9 %fusion.4 = f32[384,1024]{1,0:T(8,128)S(1)} fusion(bf16[384,4096]{1,0:T(8,128)(2,1)} %all-gather.2.cloned.1.call-done, bf16[4096,1024]{1,0:T(8,128)(2,1)} %param.12, s32[1024]{0:T(1024)S(1)} %convert_xor_fusion.1, s32[4096]{0:T(1024)S(1)} %convert_xor_fusion), kind=kOutput, calls=%fused_computation.7 | convolution fusion | flops 3229614080 | bytes 13127680 | tf_op jit(solution)/shard_map/dot_general | solution.py:48
  64.9 0.1 collective-permute-start
  65.0 3.4 %collective-permute-done = f32[384,1024]{1,0:T(8,128)S(1)} collective-permute-done((f32[384,1024]{1,0:T(8,128)S(1)}, f32[384,1024]{1,0:T(8,128)S(1)}, u32[]{:S(2)}, u32[]{:S(2)}) %collective-permute-start) | collective-permute-done | bytes 1572896 | tf_op jit(solution)/shard_map/ppermute | solution.py:54
  68.4 0.3 add.82
  68.7 0.9 collective-permute-start.1
  69.6 35.6 %collective-permute-done.1 = f32[384,1024]{1,0:T(8,128)S(1)} collective-permute-done((f32[384,1024]{1,0:T(8,128)S(1)}, f32[384,1024]{1,0:T(8,128)S(1)}, u32[]{:S(2)}, u32[]{:S(2)}) %collective-permute-start.1) | collective-permute-done | bytes 1572896 | tf_op jit(solution)/shard_map/ppermute | solution.py:54
  105.2 0.4 add.83
  105.6 1.5 collective-permute-start.2
  107.1 35.7 %collective-permute-done.2 = f32[384,1024]{1,0:T(8,128)S(1)} collective-permute-done((f32[384,1024]{1,0:T(8,128)S(1)}, f32[384,1024]{1,0:T(8,128)S(1)}, u32[]{:S(2)}, u32[]{:S(2)}) %collective-permute-start.2) | collective-permute-done | bytes 1572896 | tf_op jit(solution)/shard_map/ppermute | solution.py:54
  142.8 0.4 add.84
  143.2 1.6 collective-permute-start.3
  144.8 33.2 %collective-permute-done.3 = f32[384,1024]{1,0:T(8,128)S(1)} collective-permute-done((f32[384,1024]{1,0:T(8,128)S(1)}, f32[384,1024]{1,0:T(8,128)S(1)}, u32[]{:S(2)}, u32[]{:S(2)}) %collective-permute-start.3) | collective-permute-done | bytes 1572896 | tf_op jit(solution)/shard_map/ppermute | solution.py:54
  178.0 0.3 add.85
  178.2 3.1 %collective-permute-start.4 = (f32[384,1024]{1,0:T(8,128)S(1)}, f32[384,1024]{1,0:T(8,128)S(1)}, u32[]{:S(2)}, u32[]{:S(2)}) collective-permute-start(f32[384,1024]{1,0:T(8,128)S(1)} %add.85), channel_id=1, source_target_pairs={{0,16},{1,17},{2,18},{3,19},{4,20},{5,21},{6,22},{7,23},{8,24},{9,... | collective-permute-start | bytes 4718600 | tf_op jit(solution)/shard_map/ppermute | solution.py:54
  181.3 0.1 reshape.52
  181.5 0.3 fusion.12
  181.8 0.3 fusion.11
  182.1 0.6 fusion.10
  182.7 0.6 fusion.9
  183.3 30.5 %collective-permute-done.4 = f32[384,1024]{1,0:T(8,128)S(1)} collective-permute-done((f32[384,1024]{1,0:T(8,128)S(1)}, f32[384,1024]{1,0:T(8,128)S(1)}, u32[]{:S(2)}, u32[]{:S(2)}) %collective-permute-start.4) | collective-permute-done | bytes 1572896 | tf_op jit(solution)/shard_map/ppermute | solution.py:54
  213.9 0.7 fusion.19
  (19 shorter events, 0.2 us)
Async XLA Ops:
  6.5 50.5 %all-gather.2.cloned.1.call-start = ((), (), s32[]{:S(2)}) async-start(), calls=%async_computation | async-start | bytes 3538944 | tf_op jit(solution)/shard_map/all_gather | solution.py:49
  64.9 3.5 %collective-permute-start = (f32[384,1024]{1,0:T(8,128)S(1)}, f32[384,1024]{1,0:T(8,128)S(1)}, u32[]{:S(2)}, u32[]{:S(2)}) collective-permute-start(f32[384,1024]{1,0:T(8,128)S(1)} %fusion.4), channel_id=1, source_target_pairs={{0,1},{1,0},{2,3},{3,2},{4,5},{5,4},{6,7},{7,6},{8,9},{9,8},{10,11... | collective-permute-start | bytes 4718600 | tf_op jit(solution)/shard_map/ppermute | solution.py:54
  68.7 36.5 %collective-permute-start.1 = (f32[384,1024]{1,0:T(8,128)S(1)}, f32[384,1024]{1,0:T(8,128)S(1)}, u32[]{:S(2)}, u32[]{:S(2)}) collective-permute-start(f32[384,1024]{1,0:T(8,128)S(1)} %add.82), channel_id=1, source_target_pairs={{0,2},{1,3},{2,0},{3,1},{4,6},{5,7},{6,4},{7,5},{8,10},{9,11},{10,... | collective-permute-start | bytes 4718600 | tf_op jit(solution)/shard_map/ppermute | solution.py:54
  105.6 37.2 %collective-permute-start.2 = (f32[384,1024]{1,0:T(8,128)S(1)}, f32[384,1024]{1,0:T(8,128)S(1)}, u32[]{:S(2)}, u32[]{:S(2)}) collective-permute-start(f32[384,1024]{1,0:T(8,128)S(1)} %add.83), channel_id=1, source_target_pairs={{0,4},{1,5},{2,6},{3,7},{4,0},{5,1},{6,2},{7,3},{8,12},{9,13},{10,... | collective-permute-start | bytes 4718600 | tf_op jit(solution)/shard_map/ppermute | solution.py:54
  143.1 38.2 %copy-start.1 = (f32[200]{0:T(256)S(1)}, f32[200]{0:T(256)}, u32[]{:S(2)}) copy-start(f32[200]{0:T(256)} %param.20) | copy-start | bytes 2404
  143.1 38.3 %copy-start = (f32[2400]{0:T(1024)S(1)}, f32[2400]{0:T(1024)}, u32[]{:S(2)}) copy-start(f32[2400]{0:T(1024)} %param.21) | copy-start | bytes 28804
  143.2 38.3 %copy-start.2 = (s32[12]{0:T(128)S(1)}, s32[12]{0:T(128)}, u32[]{:S(2)}) copy-start(s32[12]{0:T(128)} %param.18) | copy-start | bytes 148
  143.2 38.3 %copy-start.3 = (s32[12]{0:T(128)S(1)}, s32[12]{0:T(128)}, u32[]{:S(2)}) copy-start(s32[12]{0:T(128)} %param.17) | copy-start | bytes 148
  143.2 34.8 %collective-permute-start.3 = (f32[384,1024]{1,0:T(8,128)S(1)}, f32[384,1024]{1,0:T(8,128)S(1)}, u32[]{:S(2)}, u32[]{:S(2)}) collective-permute-start(f32[384,1024]{1,0:T(8,128)S(1)} %add.84), channel_id=1, source_target_pairs={{0,8},{1,9},{2,10},{3,11},{4,12},{5,13},{6,14},{7,15},{8,0},{9,1},... | collective-permute-start | bytes 4718600 | tf_op jit(solution)/shard_map/ppermute | solution.py:54
  178.2 35.6 %collective-permute-start.4 = (f32[384,1024]{1,0:T(8,128)S(1)}, f32[384,1024]{1,0:T(8,128)S(1)}, u32[]{:S(2)}, u32[]{:S(2)}) collective-permute-start(f32[384,1024]{1,0:T(8,128)S(1)} %add.85), channel_id=1, source_target_pairs={{0,16},{1,17},{2,18},{3,19},{4,20},{5,21},{6,22},{7,23},{8,24},{9,... | collective-permute-start | bytes 4718600 | tf_op jit(solution)/shard_map/ppermute | solution.py:54
Sparse Core Ops, SparseCore 0:
  9.1 47.8 all-gather.1
